TPU v7x, 128 devices: a whole 4x4x4 slice. The times are simulated.
128 devices in a mesh: rows: 16 (over x, z), cols: 8 (over y, core).
Axes of the slice: x: 4, y: 4, z: 4, core: 2. Of those that a mesh axis runs over, the one named last changes fastest.
Arguments:
- counts: int32 [2048, 512, 512], P(('rows', 'cols')), may hold values from 0 to 1024, as said below
- shard_rows: int32 [2048], P(('rows', 'cols')), may hold values from 0 to 255, as said below
- shard_cols: int32 [2048], P(('rows', 'cols')), may hold values from 0 to 255, as said below
- listed: int32 [128], P(('rows', 'cols')), may hold values from 2 to 16, as said below
- row_embed: float32 [131072, 256], P(('rows', 'cols')), may hold values from -1.5 to 1.5
- row_accum: float32 [131072, 256], P(('rows', 'cols')), may hold values from 300 to 10000
- row_offset: bfloat16 [131072], P(('rows', 'cols')), may hold values from -3 to -1
- col_embed: float32 [131072, 256], P(('rows', 'cols')), may hold values from -1.5 to 1.5
- col_accum: float32 [131072, 256], P(('rows', 'cols')), may hold values from 300 to 10000
- col_offset: bfloat16 [131072], P(('rows', 'cols')), may hold values from -3 to -1
Outputs:
- row_trained: float32 [131072, 256], P(('rows', 'cols'))
- col_trained: float32 [131072, 256], P(('rows', 'cols'))
Inputs may be any that keep to these rules, and one draw needn't show every extreme that they name: `shard_rows`: entry q belongs to holder h = q // 16, the device at rows index h // 8 and cols index h % 8. Row block g is owned by device g // 2 in the same order. The row block of a listed entry is owned by a device with its holder's cols index; the listed entries of one holder use at most 1 different row blocks of any one owner, and in some holder exactly 1 of each of the 16 owners with its cols index. `shard_cols`: column block c is owned by device c // 2. The column block of a listed entry is owned by a device with its holder's rows index. No holder lists the same pair of blocks twice. The listed entries of holder h are its first listed[h] ones; its other entries and their counts take no part. `counts`: zero where the pair of items never occurs together.
All inputs are finite; a program needn't handle non-finite values.
Results may differ from a plain program's by a relative error of at most 0.0014.
Values may be sent and summed in bfloat16 or wider, within the bound.
A program may use at most 192 MiB of HBM per device.

v0:
```python
import jax
import jax.numpy as jnp
from jax import lax
from jax.sharding import PartitionSpec as P

learning_rate = 0.5
conf_base = 0.1
conf_scale = 0.25
shard_group = 4


def slopes(cell_counts, scores, row_shift, col_shift):
    floored = jnp.maximum(cell_counts, 1).astype(jnp.float32)
    pointwise = jnp.log(floored) + row_shift[:, :, None] + col_shift[:, None, :]
    weight = conf_base + conf_scale * jnp.sqrt(floored)
    return jnp.where(
        cell_counts > 0, weight * (scores - pointwise), jax.nn.sigmoid(scores - pointwise)
    )


def process(
    count_tiles, live_count, row_pool, row_shifts, row_index, col_pool, col_shifts, col_index
):
    turns = count_tiles.shape[0] // shard_group

    def one_turn(turn_index, totals):
        row_grad, col_grad = totals
        first = turn_index * shard_group
        tile_group = lax.dynamic_slice_in_dim(count_tiles, first, shard_group, 0)
        row_slots = lax.dynamic_slice_in_dim(row_index, first, shard_group, 0)
        col_slots = lax.dynamic_slice_in_dim(col_index, first, shard_group, 0)
        row_vectors = jnp.take(row_pool, row_slots, axis=0)
        col_vectors = jnp.take(col_pool, col_slots, axis=0)
        scores = jnp.einsum(
            "sbd,sed->sbe", row_vectors, col_vectors, preferred_element_type=jnp.float32
        )
        row_shift = jnp.take(row_shifts, row_slots, axis=0).astype(jnp.float32)
        col_shift = jnp.take(col_shifts, col_slots, axis=0).astype(jnp.float32)
        slope_full = slopes(tile_group, scores, row_shift, col_shift)
        in_list = first + jnp.arange(shard_group, dtype=jnp.int32) < live_count
        slope_full = jnp.where(in_list[:, None, None], slope_full, jnp.zeros_like(slope_full))
        slope_half = slope_full.astype(jnp.bfloat16)
        row_terms = jnp.einsum(
            "sbe,sed->sbd", slope_half, col_vectors, preferred_element_type=jnp.float32
        )
        col_terms = jnp.einsum(
            "sbe,sbd->sed", slope_half, row_vectors, preferred_element_type=jnp.float32
        )
        return (row_grad.at[row_slots].add(row_terms), col_grad.at[col_slots].add(col_terms))

    start = (jnp.zeros(row_pool.shape, jnp.float32), jnp.zeros(col_pool.shape, jnp.float32))
    return lax.fori_loop(0, turns, one_turn, start)


def on_device(
    counts,
    shard_rows,
    shard_cols,
    listed,
    row_embed,
    row_accum,
    row_offset,
    col_embed,
    col_accum,
    col_offset,
):
    block_items = counts.shape[1]
    features = row_embed.shape[1]
    row_owned = row_embed.shape[0] // block_items
    col_owned = col_embed.shape[0] // block_items
    col_devices = lax.axis_size("cols")
    live_count = listed[0]
    row_set = shard_rows // row_owned // col_devices * row_owned + shard_rows % row_owned
    col_set = shard_cols // col_owned % col_devices * col_owned + shard_cols % col_owned
    row_half = row_embed.astype(jnp.bfloat16)
    col_half = col_embed.astype(jnp.bfloat16)
    col_pool = lax.all_gather(col_half, "cols", axis=0, tiled=True)
    col_shifts = lax.all_gather(col_offset, "cols", axis=0, tiled=True)
    row_pool = lax.all_gather(row_half, "rows", axis=0, tiled=True)
    row_shifts = lax.all_gather(row_offset, "rows", axis=0, tiled=True)
    row_pool = row_pool.reshape(-1, block_items, features)
    row_shifts = row_shifts.reshape(-1, block_items)
    row_part, col_part = process(
        counts,
        live_count,
        row_pool,
        row_shifts,
        row_set,
        col_pool.reshape(-1, block_items, features),
        col_shifts.reshape(-1, block_items),
        col_set,
    )
    row_grad = lax.psum_scatter(
        row_part.reshape(-1, features), "rows", scatter_dimension=0, tiled=True
    )
    col_grad = lax.psum_scatter(
        col_part.reshape(-1, features), "cols", scatter_dimension=0, tiled=True
    )
    row_accum = row_accum + row_grad * row_grad
    col_accum = col_accum + col_grad * col_grad
    row_embed = row_embed - learning_rate * row_grad / jnp.sqrt(row_accum)
    col_embed = col_embed - learning_rate * col_grad / jnp.sqrt(col_accum)
    return (row_embed, col_embed)


def solution(mesh):
    in_specs = (
        P(("rows", "cols"), None, None),
        P(("rows", "cols")),
        P(("rows", "cols")),
        P(("rows", "cols")),
        P(("rows", "cols"), None),
        P(("rows", "cols"), None),
        P(("rows", "cols")),
        P(("rows", "cols"), None),
        P(("rows", "cols"), None),
        P(("rows", "cols")),
    )
    out_specs = (P(("rows", "cols"), None), P(("rows", "cols"), None))
    return jax.shard_map(
        on_device, mesh=mesh, in_specs=in_specs, out_specs=out_specs, check_vma=False
    )
```

profile of v0, /device:TPU:1, one launch (start us, length us, event | category | flops | bytes accessed | tf_op | source)
XLA Modules:
  0.0 412.7 jit_solution(9346505922726020721)
XLA Ops:
  11.6 13.5 %all_gather.15 = bf16[8192]{0:T(1024)(128)(2,1)S(1)} all-gather(bf16[1024]{0:T(1024)(128)(2,1)S(1)} %copy-done.3), channel_id=1, replica_groups=mesh['rows'=16,'cols'=8] {'cols'}, dimensions={0}, use_global_device_ids=true | all-gather | bytes 18432 | tf_op jit(solution)/shard_map/all_gather | solution.py:78
  25.1 21.2 %all_gather.14 = bf16[16384]{0:T(1024)(128)(2,1)S(1)} all-gather(bf16[1024]{0:T(1024)(128)(2,1)S(1)} %copy-done.4), channel_id=1, replica_groups=mesh['rows'=16,'cols'=8] {'rows'}, dimensions={0}, use_global_device_ids=true | all-gather | bytes 34816 | tf_op jit(solution)/shard_map/all_gather | solution.py:80
  46.4 72.6 %all-gather.3.cloned.1.call-done = bf16[16384,256]{1,0:T(8,128)(2,1)} async-done(((bf16[1024,256]{1,0:T(8,128)(2,1)}), bf16[16384,256]{1,0:T(8,128)(2,1)}) %all-gather.3.cloned.1.call-update) | async-done | bytes 8388624 | tf_op jit(solution)/shard_map/all_gather | solution.py:79
  119.0 4.1 broadcast_in_dim.102
  123.2 7.7 %broadcast_in_dim.101 = f32[32,512,256]{2,1,0:T(8,128)} broadcast(f32[]{:T(128)} %constant.184.clone.1), dimensions={} | broadcast | bytes 16777220 | tf_op jit(solution)/shard_map/broadcast_in_dim | solution.py:51
  130.9 106.7 %while.15 = (s32[]{:T(128)}, f32[32,512,256]{2,1,0:T(8,128)}, f32[16,512,256]{2,1,0:T(8,128)}, s32[16]{0:T(128)S(1)}, s32[]{:T(128)}, /*index=5*/s32[16,512,512]...) while((s32[]{:T(128)}, f32[32,512,256]{2,1,0:T(8,128)}, ...), condition=%wide.region_3.4_spmd, body=%wide.region_0.3_spmd.sunk | while | flops 1629497344 | bytes 35717552 | solution.py:52
  132.9 4.0 gather_fusion.2
  136.9 2.8 gather_fusion.3
  139.7 5.6 %select_convert_fusion.8 = bf16[4,512,512]{2,1,0:T(8,128)(2,1)S(1)} fusion(s32[16,512,512]{2,1,0:T(8,128)} %get-tuple-element.329, s32[]{:T(128)S(6)} %select_n.171, f32[4,512]{1,0:T(4,128)S(1)} %select_convert_fusion.6, f32[4,512]{1,0:T(4,128)S(1)} %select_convert_fusion.7, pred[4]{0:T(512)(128)(4,1)S(1)} %add_compare_fusion.2, ...), kind=kOutput, calls=%fused_computation.6.clone.1 | convolution fusion | flops 553648128 | bytes 8405008 | tf_op jit(solution)/shard_map/while/body/eval_jaxpr/sbd,sed->sbe/dot_general | solution.py:34
  145.3 2.2 fusion.18
  148.3 4.9 %scatter_fusion.1 = f32[16,512,256]{2,1,0:T(8,128)} fusion(f32[16,512,256]{2,1,0:T(8,128)} %get-tuple-element.311, s32[4]{0:T(128)S(1)} %get-tuple-element.291, f32[4,512,256]{2,1,0:T(8,128)} %fusion.18), kind=kCustom, calls=%fused_computation.5.clone.1 | custom fusion | flops 524288 | bytes 6291472 | tf_op jit(solution)/shard_map/while/body/eval_jaxpr/scatter-add | solution.py:49
  153.2 4.2 %scatter_fusion = f32[32,512,256]{2,1,0:T(8,128)} fusion(f32[32,512,256]{2,1,0:T(8,128)} %get-tuple-element.310, s32[4]{0:T(128)S(1)} %get-tuple-element.290, f32[4,512,256]{2,1,0:T(8,128)S(1)} %fusion.17), kind=kCustom, calls=%fused_computation.4.clone.1 | custom fusion | flops 524288 | bytes 6291472 | tf_op jit(solution)/shard_map/while/body/eval_jaxpr/scatter-add | solution.py:49
  159.5 4.0 gather_fusion.2
  163.5 2.8 gather_fusion.3
  166.3 5.6 %select_convert_fusion.8 = bf16[4,512,512]{2,1,0:T(8,128)(2,1)S(1)} fusion(s32[16,512,512]{2,1,0:T(8,128)} %get-tuple-element.329, s32[]{:T(128)S(6)} %select_n.171, f32[4,512]{1,0:T(4,128)S(1)} %select_convert_fusion.6, f32[4,512]{1,0:T(4,128)S(1)} %select_convert_fusion.7, pred[4]{0:T(512)(128)(4,1)S(1)} %add_compare_fusion.2, ...), kind=kOutput, calls=%fused_computation.6.clone.1 | convolution fusion | flops 553648128 | bytes 8405008 | tf_op jit(solution)/shard_map/while/body/eval_jaxpr/sbd,sed->sbe/dot_general | solution.py:34
  171.9 2.2 fusion.18
  174.9 5.0 %scatter_fusion.1 = f32[16,512,256]{2,1,0:T(8,128)} fusion(f32[16,512,256]{2,1,0:T(8,128)} %get-tuple-element.311, s32[4]{0:T(128)S(1)} %get-tuple-element.291, f32[4,512,256]{2,1,0:T(8,128)} %fusion.18), kind=kCustom, calls=%fused_computation.5.clone.1 | custom fusion | flops 524288 | bytes 6291472 | tf_op jit(solution)/shard_map/while/body/eval_jaxpr/scatter-add | solution.py:49
  179.9 4.2 %scatter_fusion = f32[32,512,256]{2,1,0:T(8,128)} fusion(f32[32,512,256]{2,1,0:T(8,128)} %get-tuple-element.310, s32[4]{0:T(128)S(1)} %get-tuple-element.290, f32[4,512,256]{2,1,0:T(8,128)S(1)} %fusion.17), kind=kCustom, calls=%fused_computation.4.clone.1 | custom fusion | flops 524288 | bytes 6291472 | tf_op jit(solution)/shard_map/while/body/eval_jaxpr/scatter-add | solution.py:49
  186.2 4.0 gather_fusion.2
  190.2 2.8 gather_fusion.3
  193.1 5.6 %select_convert_fusion.8 = bf16[4,512,512]{2,1,0:T(8,128)(2,1)S(1)} fusion(s32[16,512,512]{2,1,0:T(8,128)} %get-tuple-element.329, s32[]{:T(128)S(6)} %select_n.171, f32[4,512]{1,0:T(4,128)S(1)} %select_convert_fusion.6, f32[4,512]{1,0:T(4,128)S(1)} %select_convert_fusion.7, pred[4]{0:T(512)(128)(4,1)S(1)} %add_compare_fusion.2, ...), kind=kOutput, calls=%fused_computation.6.clone.1 | convolution fusion | flops 553648128 | bytes 8405008 | tf_op jit(solution)/shard_map/while/body/eval_jaxpr/sbd,sed->sbe/dot_general | solution.py:34
  201.6 5.0 %scatter_fusion.1 = f32[16,512,256]{2,1,0:T(8,128)} fusion(f32[16,512,256]{2,1,0:T(8,128)} %get-tuple-element.311, s32[4]{0:T(128)S(1)} %get-tuple-element.291, f32[4,512,256]{2,1,0:T(8,128)} %fusion.18), kind=kCustom, calls=%fused_computation.5.clone.1 | custom fusion | flops 524288 | bytes 6291472 | tf_op jit(solution)/shard_map/while/body/eval_jaxpr/scatter-add | solution.py:49
  206.6 4.3 %scatter_fusion = f32[32,512,256]{2,1,0:T(8,128)} fusion(f32[32,512,256]{2,1,0:T(8,128)} %get-tuple-element.310, s32[4]{0:T(128)S(1)} %get-tuple-element.290, f32[4,512,256]{2,1,0:T(8,128)S(1)} %fusion.17), kind=kCustom, calls=%fused_computation.4.clone.1 | custom fusion | flops 524288 | bytes 6291472 | tf_op jit(solution)/shard_map/while/body/eval_jaxpr/scatter-add | solution.py:49
  213.0 4.0 gather_fusion.2
  217.0 2.8 gather_fusion.3
  219.8 5.6 %select_convert_fusion.8 = bf16[4,512,512]{2,1,0:T(8,128)(2,1)S(1)} fusion(s32[16,512,512]{2,1,0:T(8,128)} %get-tuple-element.329, s32[]{:T(128)S(6)} %select_n.171, f32[4,512]{1,0:T(4,128)S(1)} %select_convert_fusion.6, f32[4,512]{1,0:T(4,128)S(1)} %select_convert_fusion.7, pred[4]{0:T(512)(128)(4,1)S(1)} %add_compare_fusion.2, ...), kind=kOutput, calls=%fused_computation.6.clone.1 | convolution fusion | flops 553648128 | bytes 8405008 | tf_op jit(solution)/shard_map/while/body/eval_jaxpr/sbd,sed->sbe/dot_general | solution.py:34
  228.4 5.0 %scatter_fusion.1 = f32[16,512,256]{2,1,0:T(8,128)} fusion(f32[16,512,256]{2,1,0:T(8,128)} %get-tuple-element.311, s32[4]{0:T(128)S(1)} %get-tuple-element.291, f32[4,512,256]{2,1,0:T(8,128)} %fusion.18), kind=kCustom, calls=%fused_computation.5.clone.1 | custom fusion | flops 524288 | bytes 6291472 | tf_op jit(solution)/shard_map/while/body/eval_jaxpr/scatter-add | solution.py:49
  233.4 4.2 %scatter_fusion = f32[32,512,256]{2,1,0:T(8,128)} fusion(f32[32,512,256]{2,1,0:T(8,128)} %get-tuple-element.310, s32[4]{0:T(128)S(1)} %get-tuple-element.290, f32[4,512,256]{2,1,0:T(8,128)S(1)} %fusion.17), kind=kCustom, calls=%fused_computation.4.clone.1 | custom fusion | flops 524288 | bytes 6291472 | tf_op jit(solution)/shard_map/while/body/eval_jaxpr/scatter-add | solution.py:49
  238.2 51.2 %reduce-scatter.5.cloned.1.call-done = f32[1024,256]{1,0:T(8,128)} async-done(((f32[8192,256]{1,0:T(8,128)}), f32[1024,256]{1,0:T(8,128)}) %reduce-scatter.5.cloned.1.call-update) | async-done | bytes 1048592 | tf_op jit(solution)/shard_map/reduce_scatter | solution.py:96
  289.4 2.4 multiply_subtract_fusion
  291.8 111.7 %reduce-scatter.3.cloned.1.call-done = f32[1024,256]{1,0:T(8,128)} async-done(((f32[16384,256]{1,0:T(8,128)}), f32[1024,256]{1,0:T(8,128)}) %reduce-scatter.3.cloned.1.call-update) | async-done | bytes 1048592 | tf_op jit(solution)/shard_map/reduce_scatter | solution.py:93
  403.5 2.7 multiply_subtract_fusion.1
  (66 shorter events, 20.7 us)
Async XLA Ops:
  7.2 4.4 %copy-start.3 = (bf16[1024]{0:T(1024)(128)(2,1)S(1)}, bf16[1024]{0:T(1024)(128)(2,1)}, u32[]{:S(2)}) copy-start(bf16[1024]{0:T(1024)(128)(2,1)} %param.21) | copy-start | bytes 6148
  7.2 17.9 %copy-start.4 = (bf16[1024]{0:T(1024)(128)(2,1)S(1)}, bf16[1024]{0:T(1024)(128)(2,1)}, u32[]{:S(2)}) copy-start(bf16[1024]{0:T(1024)(128)(2,1)} %param.18) | copy-start | bytes 6148
  7.2 39.2 %copy-start.6 = (s32[16]{0:T(128)S(1)}, s32[16]{0:T(128)}, u32[]{:S(2)}) copy-start(s32[16]{0:T(128)} %param.14) | copy-start | bytes 196
  7.2 39.2 %copy-start.5 = (s32[16]{0:T(128)S(1)}, s32[16]{0:T(128)}, u32[]{:S(2)}) copy-start(s32[16]{0:T(128)} %param.13) | copy-start | bytes 196
  7.2 39.2 %all-gather.5.cloned.1.call-start = ((), (), s32[]{:S(2)}) async-start(), calls=%async_computation.3 | async-start | bytes 4718592 | tf_op jit(solution)/shard_map/all_gather | solution.py:77
  9.3 109.7 %all-gather.3.cloned.1.call-start = ((), (), s32[]{:S(2)}) async-start(), calls=%async_computation.2 | async-start | bytes 8912896 | tf_op jit(solution)/shard_map/all_gather | solution.py:79
  11.5 277.9 %reduce-scatter.5.cloned.1.call-start = ((), (), s32[]{:S(2)}) async-start(), calls=%async_computation.5 | async-start | bytes 9437184 | tf_op jit(solution)/shard_map/reduce_scatter | solution.py:96
  237.6 165.8 %reduce-scatter.3.cloned.1.call-start = ((), (), s32[]{:S(2)}) async-start(), calls=%async_computation.4 | async-start | bytes 17825792 | tf_op jit(solution)/shard_map/reduce_scatter | solution.py:93
  237.7 51.7 %copy-start = (f32[1024,256]{1,0:T(8,128)S(1)}, f32[1024,256]{1,0:T(8,128)}, u32[]{:S(2)}) copy-start(f32[1024,256]{1,0:T(8,128)} %param.19) | copy-start | bytes 3145732
  237.7 51.7 %copy-start.2 = (f32[1024,256]{1,0:T(8,128)S(1)}, f32[1024,256]{1,0:T(8,128)}, u32[]{:S(2)}) copy-start(f32[1024,256]{1,0:T(8,128)} %param.20) | copy-start | bytes 3145732
  238.2 165.3 %copy-start.1 = (f32[1024,256]{1,0:T(8,128)S(1)}, f32[1024,256]{1,0:T(8,128)}, u32[]{:S(2)}) copy-start(f32[1024,256]{1,0:T(8,128)} %param.16) | copy-start | bytes 3145732
Sparse Core Ops, SparseCore 0:
  10.3 35.6 all-gather.4
  48.7 70.2 all-gather.2
  237.7 51.6 reduce-scatter.4
  292.7 110.7 reduce-scatter.2
where the time goes:
time: 413 us
  waiting for transfers between devices  236 us (57%)
  other arithmetic  49.8 us (12%)
  local copies, waits for them, and re-layouts  43.6 us (11%)
  blocking collectives  34.7 us (8%)
  matrix products  34.3 us (8%)
  between operations  13.9 us (3%)
    reduce_scatter x1, waiting for transfers between devices, on_device(): lax.psum_scatter(row_part.reshape(-1, features), 'rows', scatter_dimensio...  112 us
    all_gather x1, waiting for transfers between devices, on_device(): row_pool = lax.all_gather(row_half, 'rows', axis=0, tiled=True)  72.6 us
    reduce_scatter x1, waiting for transfers between devices, on_device(): lax.psum_scatter(col_part.reshape(-1, features), 'cols', scatter_dimensio...  51.2 us
    dot_general x4, matrix products, one_turn(): jnp.einsum('sbd,sed->sbe', row_vectors, col_vectors, preferred_element_ty...  22.3 us
    all_gather x1, blocking collectives, on_device(): row_shifts = lax.all_gather(row_offset, 'rows', axis=0, tiled=True)  21.2 us
    scatter-add x4, other arithmetic, one_turn(): col_grad.at[col_slots].add(col_terms)  19.9 us
    scatter-add x4, other arithmetic, one_turn(): row_grad.at[row_slots].add(row_terms)  17 us
    gather x4, local copies, waits for them, and re-layouts, one_turn(): row_vectors = jnp.take(row_pool, row_slots, axis=0)  16 us
  transfers between devices with their start and end apart: 4, of which 3 were waited for; matrix products, arithmetic and copies ran while one was open for 1% of the time, Pallas kernels for 0%

commit v1 on v0

--- a/solution.py
+++ b/solution.py
@@ -77,7 +77,19 @@
     col_pool = lax.all_gather(col_half, "cols", axis=0, tiled=True)
     col_shifts = lax.all_gather(col_offset, "cols", axis=0, tiled=True)
     row_pool = lax.all_gather(row_half, "rows", axis=0, tiled=True)
-    row_shifts = lax.all_gather(row_offset, "rows", axis=0, tiled=True)
+    world = lax.axis_size("rows")
+    by_place = tuple(((j, (j + 1) % world) for j in range(world)))
+    blocks_here = tuple(((j, (j - 1) % world) for j in range(world)))
+    newest, value_now = ([row_offset], [row_offset])
+    for _ in range(world // 2):
+        mid_arr = lax.ppermute(newest[-1], axis_name="rows", perm=by_place)
+        newest.append(mid_arr)
+    for _ in tuple(range((world - 1) // 2)):
+        z_new = lax.ppermute(value_now[-1], axis_name="rows", perm=blocks_here)
+        value_now.append(z_new)
+    reply = jnp.concatenate([*newest[::-1], *value_now[1:]], 0)
+    top = lax.axis_index("rows")
+    row_shifts = jnp.roll(reply, shift=(top - world // 2) * row_offset.shape[0], axis=0)
     row_pool = row_pool.reshape(-1, block_items, features)
     row_shifts = row_shifts.reshape(-1, block_items)
     row_part, col_part = process(

time: 413 us -> 413 us (level)
  starting transfers between devices: 0.16 us -> 36.9 us
  waiting for transfers between devices: 236 us -> 213 us
  blocking collectives: 34.7 us -> 20.4 us
    ppermute x0 -> x15, starting transfers between devices: none -> 36.8 us  [the longest x7 34.2 us: on_device(): z_new = lax.ppermute(value_now[-1], axis_name='rows', perm=blocks_here)]
    all_gather x1, waiting for transfers between devices: 72.6 us -> 38.3 us  [on_device(): row_pool = lax.all_gather(row_half, 'rows', axis=0, tiled=True)]
    all_gather x1 -> x0, blocking collectives: 21.2 us -> none  [on_device(): row_shifts = lax.all_gather(row_offset, 'rows', axis=0, tiled=True)]
    ppermute x0 -> x15, waiting for transfers between devices: none -> 11.4 us  [the longest x8 10.8 us: on_device(): mid_arr = lax.ppermute(newest[-1], axis_name='rows', perm=by_place)]
    all_gather x1, blocking collectives: 13.5 us -> 20.4 us  [on_device(): col_shifts = lax.all_gather(col_offset, 'cols', axis=0, tiled=True)]
  transfers between devices with their start and end apart: 4 -> 19, of which waited for: 3 -> 11; matrix products, arithmetic and copies ran while one was open for 1% -> 1% of each run, Pallas kernels for 0% -> 0%
where the time goes in v1:
time: 413 us; the launch traced here: 412 us
  waiting for transfers between devices  213 us (52%)
  other arithmetic  49.8 us (12%)
  local copies, waits for them, and re-layouts  43.9 us (11%)
  starting transfers between devices  36.9 us (9%)
  matrix products  34.3 us (8%)
  blocking collectives  20.4 us (5%)
  between operations  14 us (3%)
    reduce_scatter x1, waiting for transfers between devices, on_device(): lax.psum_scatter(row_part.reshape(-1, features), 'rows', scatter_dimensio...  112 us
    reduce_scatter x1, waiting for transfers between devices, on_device(): lax.psum_scatter(col_part.reshape(-1, features), 'cols', scatter_dimensio...  51 us
    all_gather x1, waiting for transfers between devices, on_device(): row_pool = lax.all_gather(row_half, 'rows', axis=0, tiled=True)  38.3 us
    ppermute x7, starting transfers between devices, on_device(): z_new = lax.ppermute(value_now[-1], axis_name='rows', perm=blocks_here)  34.2 us
    dot_general x4, matrix products, one_turn(): jnp.einsum('sbd,sed->sbe', row_vectors, col_vectors, preferred_element_ty...  22.3 us
    all_gather x1, blocking collectives, on_device(): col_shifts = lax.all_gather(col_offset, 'cols', axis=0, tiled=True)  20.4 us
    scatter-add x4, other arithmetic, one_turn(): col_grad.at[col_slots].add(col_terms)  19.9 us
    scatter-add x4, other arithmetic, one_turn(): row_grad.at[row_slots].add(row_terms)  17 us
  transfers between devices with their start and end apart: 19, of which 11 were waited for; matrix products, arithmetic and copies ran while one was open for 1% of the time, Pallas kernels for 0%

profile of v1, /device:TPU:1, one launch (start us, length us, event | category | flops | bytes accessed | tf_op | source)
XLA Modules:
  0.0 412.5 jit_solution(5187968068382129802)
XLA Ops:
  14.1 5.3 %collective-permute-done = bf16[1024]{0:T(1024)(128)(2,1)S(1)} collective-permute-done((bf16[1024]{0:T(1024)(128)(2,1)S(1)}, bf16[1024]{0:T(1024)(128)(2,1)S(1)}, u32[]{:S(2)}, u32[]{:S(2)}) %collective-permute-start) | collective-permute-done | bytes 2080 | tf_op jit(solution)/shard_map/ppermute | solution.py:85
  19.4 4.8 %collective-permute-start.8 = (bf16[1024]{0:T(1024)(128)(2,1)S(1)}, bf16[1024]{0:T(1024)(128)(2,1)S(1)}, u32[]{:S(2)}, u32[]{:S(2)}) collective-permute-start(bf16[1024]{0:T(1024)(128)(2,1)S(1)} %copy-done.3), channel_id=1, source_target_pairs={{0,120},{8,0},{16,8},{24,16},{32,24},{40,32},{48,40},{56,48},{64,5... | collective-permute-start | bytes 6152 | tf_op jit(solution)/shard_map/ppermute | solution.py:88
  25.1 4.8 %collective-permute-start.9 = (bf16[1024]{0:T(1024)(128)(2,1)S(1)}, bf16[1024]{0:T(1024)(128)(2,1)S(1)}, u32[]{:S(2)}, u32[]{:S(2)}) collective-permute-start(bf16[1024]{0:T(1024)(128)(2,1)S(1)} %collective-permute-done.8), channel_id=1, source_target_pairs={{0,120},{8,0},{16,8},{24,16},{32,24},{40,32},{48,40},{56,48},{64,5... | collective-permute-start | bytes 6152 | tf_op jit(solution)/shard_map/ppermute | solution.py:88
  30.9 4.8 %collective-permute-start.10 = (bf16[1024]{0:T(1024)(128)(2,1)S(1)}, bf16[1024]{0:T(1024)(128)(2,1)S(1)}, u32[]{:S(2)}, u32[]{:S(2)}) collective-permute-start(bf16[1024]{0:T(1024)(128)(2,1)S(1)} %collective-permute-done.9), channel_id=1, source_target_pairs={{0,120},{8,0},{16,8},{24,16},{32,24},{40,32},{48,40},{56,48},{64,5... | collective-permute-start | bytes 6152 | tf_op jit(solution)/shard_map/ppermute | solution.py:88
  36.6 4.8 %collective-permute-start.11 = (bf16[1024]{0:T(1024)(128)(2,1)S(1)}, bf16[1024]{0:T(1024)(128)(2,1)S(1)}, u32[]{:S(2)}, u32[]{:S(2)}) collective-permute-start(bf16[1024]{0:T(1024)(128)(2,1)S(1)} %collective-permute-done.10), channel_id=1, source_target_pairs={{0,120},{8,0},{16,8},{24,16},{32,24},{40,32},{48,40},{56,48},{64,5... | collective-permute-start | bytes 6152 | tf_op jit(solution)/shard_map/ppermute | solution.py:88
  42.4 4.8 %collective-permute-start.12 = (bf16[1024]{0:T(1024)(128)(2,1)S(1)}, bf16[1024]{0:T(1024)(128)(2,1)S(1)}, u32[]{:S(2)}, u32[]{:S(2)}) collective-permute-start(bf16[1024]{0:T(1024)(128)(2,1)S(1)} %collective-permute-done.11), channel_id=1, source_target_pairs={{0,120},{8,0},{16,8},{24,16},{32,24},{40,32},{48,40},{56,48},{64,5... | collective-permute-start | bytes 6152 | tf_op jit(solution)/shard_map/ppermute | solution.py:88
  48.2 5.0 %collective-permute-start.13 = (bf16[1024]{0:T(1024)(128)(2,1)S(1)}, bf16[1024]{0:T(1024)(128)(2,1)S(1)}, u32[]{:S(2)}, u32[]{:S(2)}) collective-permute-start(bf16[1024]{0:T(1024)(128)(2,1)S(1)} %collective-permute-done.12), channel_id=1, source_target_pairs={{0,120},{8,0},{16,8},{24,16},{32,24},{40,32},{48,40},{56,48},{64,5... | collective-permute-start | bytes 6152 | tf_op jit(solution)/shard_map/ppermute | solution.py:88
  53.9 20.4 %all_gather.11 = bf16[8192]{0:T(1024)(128)(2,1)S(1)} all-gather(bf16[1024]{0:T(1024)(128)(2,1)S(1)} %copy-done.4), channel_id=1, replica_groups=mesh['rows'=16,'cols'=8] {'cols'}, dimensions={0}, use_global_device_ids=true | all-gather | bytes 18432 | tf_op jit(solution)/shard_map/all_gather | solution.py:78
  74.4 5.3 %collective-permute-start.14 = (bf16[1024]{0:T(1024)(128)(2,1)S(1)}, bf16[1024]{0:T(1024)(128)(2,1)S(1)}, u32[]{:S(2)}, u32[]{:S(2)}) collective-permute-start(bf16[1024]{0:T(1024)(128)(2,1)S(1)} %collective-permute-done.13), channel_id=1, source_target_pairs={{0,120},{8,0},{16,8},{24,16},{32,24},{40,32},{48,40},{56,48},{64,5... | collective-permute-start | bytes 6152 | tf_op jit(solution)/shard_map/ppermute | solution.py:88
  80.7 38.3 %all-gather.3.cloned.1.call-done = bf16[16384,256]{1,0:T(8,128)(2,1)} async-done(((bf16[1024,256]{1,0:T(8,128)(2,1)}), bf16[16384,256]{1,0:T(8,128)(2,1)}) %all-gather.3.cloned.1.call-update) | async-done | bytes 8388624 | tf_op jit(solution)/shard_map/all_gather | solution.py:79
  119.1 4.1 broadcast_in_dim.102
  123.2 7.7 %broadcast_in_dim.101 = f32[32,512,256]{2,1,0:T(8,128)} broadcast(f32[]{:T(128)} %constant.208.clone.1), dimensions={} | broadcast | bytes 16777220 | tf_op jit(solution)/shard_map/broadcast_in_dim | solution.py:51
  130.9 106.7 %while.15 = (s32[]{:T(128)}, f32[32,512,256]{2,1,0:T(8,128)}, f32[16,512,256]{2,1,0:T(8,128)}, s32[16]{0:T(128)S(1)}, s32[]{:T(128)}, /*index=5*/s32[16,512,512]...) while((s32[]{:T(128)}, f32[32,512,256]{2,1,0:T(8,128)}, ...), condition=%wide.region_3.4_spmd, body=%wide.region_0.3_spmd.sunk | while | flops 1629497344 | bytes 35717552 | solution.py:52
  132.9 4.0 gather_fusion.2
  136.9 2.8 gather_fusion.3
  139.7 5.6 %select_convert_fusion.8 = bf16[4,512,512]{2,1,0:T(8,128)(2,1)S(1)} fusion(s32[16,512,512]{2,1,0:T(8,128)} %get-tuple-element.329, s32[]{:T(128)S(6)} %select_n.185, f32[4,512]{1,0:T(4,128)S(1)} %select_convert_fusion.6, f32[4,512]{1,0:T(4,128)S(1)} %select_convert_fusion.7, pred[4]{0:T(512)(128)(4,1)S(1)} %add_compare_fusion.2, ...), kind=kOutput, calls=%fused_computation.6.clone.1 | convolution fusion | flops 553648128 | bytes 8405008 | tf_op jit(solution)/shard_map/while/body/eval_jaxpr/sbd,sed->sbe/dot_general | solution.py:34
  148.3 4.9 %scatter_fusion.1 = f32[16,512,256]{2,1,0:T(8,128)} fusion(f32[16,512,256]{2,1,0:T(8,128)} %get-tuple-element.311, s32[4]{0:T(128)S(1)} %get-tuple-element.291, f32[4,512,256]{2,1,0:T(8,128)} %fusion.18), kind=kCustom, calls=%fused_computation.5.clone.1 | custom fusion | flops 524288 | bytes 6291472 | tf_op jit(solution)/shard_map/while/body/eval_jaxpr/scatter-add | solution.py:49
  153.2 4.3 %scatter_fusion = f32[32,512,256]{2,1,0:T(8,128)} fusion(f32[32,512,256]{2,1,0:T(8,128)} %get-tuple-element.310, s32[4]{0:T(128)S(1)} %get-tuple-element.290, f32[4,512,256]{2,1,0:T(8,128)S(1)} %fusion.17), kind=kCustom, calls=%fused_computation.4.clone.1 | custom fusion | flops 524288 | bytes 6291472 | tf_op jit(solution)/shard_map/while/body/eval_jaxpr/scatter-add | solution.py:49
  159.5 4.0 gather_fusion.2
  166.3 5.6 %select_convert_fusion.8 = bf16[4,512,512]{2,1,0:T(8,128)(2,1)S(1)} fusion(s32[16,512,512]{2,1,0:T(8,128)} %get-tuple-element.329, s32[]{:T(128)S(6)} %select_n.185, f32[4,512]{1,0:T(4,128)S(1)} %select_convert_fusion.6, f32[4,512]{1,0:T(4,128)S(1)} %select_convert_fusion.7, pred[4]{0:T(512)(128)(4,1)S(1)} %add_compare_fusion.2, ...), kind=kOutput, calls=%fused_computation.6.clone.1 | convolution fusion | flops 553648128 | bytes 8405008 | tf_op jit(solution)/shard_map/while/body/eval_jaxpr/sbd,sed->sbe/dot_general | solution.py:34
  174.9 5.0 %scatter_fusion.1 = f32[16,512,256]{2,1,0:T(8,128)} fusion(f32[16,512,256]{2,1,0:T(8,128)} %get-tuple-element.311, s32[4]{0:T(128)S(1)} %get-tuple-element.291, f32[4,512,256]{2,1,0:T(8,128)} %fusion.18), kind=kCustom, calls=%fused_computation.5.clone.1 | custom fusion | flops 524288 | bytes 6291472 | tf_op jit(solution)/shard_map/while/body/eval_jaxpr/scatter-add | solution.py:49
  179.9 4.2 %scatter_fusion = f32[32,512,256]{2,1,0:T(8,128)} fusion(f32[32,512,256]{2,1,0:T(8,128)} %get-tuple-element.310, s32[4]{0:T(128)S(1)} %get-tuple-element.290, f32[4,512,256]{2,1,0:T(8,128)S(1)} %fusion.17), kind=kCustom, calls=%fused_computation.4.clone.1 | custom fusion | flops 524288 | bytes 6291472 | tf_op jit(solution)/shard_map/while/body/eval_jaxpr/scatter-add | solution.py:49
  186.2 4.0 gather_fusion.2
  193.0 5.6 %select_convert_fusion.8 = bf16[4,512,512]{2,1,0:T(8,128)(2,1)S(1)} fusion(s32[16,512,512]{2,1,0:T(8,128)} %get-tuple-element.329, s32[]{:T(128)S(6)} %select_n.185, f32[4,512]{1,0:T(4,128)S(1)} %select_convert_fusion.6, f32[4,512]{1,0:T(4,128)S(1)} %select_convert_fusion.7, pred[4]{0:T(512)(128)(4,1)S(1)} %add_compare_fusion.2, ...), kind=kOutput, calls=%fused_computation.6.clone.1 | convolution fusion | flops 553648128 | bytes 8405008 | tf_op jit(solution)/shard_map/while/body/eval_jaxpr/sbd,sed->sbe/dot_general | solution.py:34
  201.6 5.1 %scatter_fusion.1 = f32[16,512,256]{2,1,0:T(8,128)} fusion(f32[16,512,256]{2,1,0:T(8,128)} %get-tuple-element.311, s32[4]{0:T(128)S(1)} %get-tuple-element.291, f32[4,512,256]{2,1,0:T(8,128)} %fusion.18), kind=kCustom, calls=%fused_computation.5.clone.1 | custom fusion | flops 524288 | bytes 6291472 | tf_op jit(solution)/shard_map/while/body/eval_jaxpr/scatter-add | solution.py:49
  206.6 4.3 %scatter_fusion = f32[32,512,256]{2,1,0:T(8,128)} fusion(f32[32,512,256]{2,1,0:T(8,128)} %get-tuple-element.310, s32[4]{0:T(128)S(1)} %get-tuple-element.290, f32[4,512,256]{2,1,0:T(8,128)S(1)} %fusion.17), kind=kCustom, calls=%fused_computation.4.clone.1 | custom fusion | flops 524288 | bytes 6291472 | tf_op jit(solution)/shard_map/while/body/eval_jaxpr/scatter-add | solution.py:49
  213.0 4.0 gather_fusion.2
  219.8 5.6 %select_convert_fusion.8 = bf16[4,512,512]{2,1,0:T(8,128)(2,1)S(1)} fusion(s32[16,512,512]{2,1,0:T(8,128)} %get-tuple-element.329, s32[]{:T(128)S(6)} %select_n.185, f32[4,512]{1,0:T(4,128)S(1)} %select_convert_fusion.6, f32[4,512]{1,0:T(4,128)S(1)} %select_convert_fusion.7, pred[4]{0:T(512)(128)(4,1)S(1)} %add_compare_fusion.2, ...), kind=kOutput, calls=%fused_computation.6.clone.1 | convolution fusion | flops 553648128 | bytes 8405008 | tf_op jit(solution)/shard_map/while/body/eval_jaxpr/sbd,sed->sbe/dot_general | solution.py:34
  228.4 5.0 %scatter_fusion.1 = f32[16,512,256]{2,1,0:T(8,128)} fusion(f32[16,512,256]{2,1,0:T(8,128)} %get-tuple-element.311, s32[4]{0:T(128)S(1)} %get-tuple-element.291, f32[4,512,256]{2,1,0:T(8,128)} %fusion.18), kind=kCustom, calls=%fused_computation.5.clone.1 | custom fusion | flops 524288 | bytes 6291472 | tf_op jit(solution)/shard_map/while/body/eval_jaxpr/scatter-add | solution.py:49
  233.4 4.2 %scatter_fusion = f32[32,512,256]{2,1,0:T(8,128)} fusion(f32[32,512,256]{2,1,0:T(8,128)} %get-tuple-element.310, s32[4]{0:T(128)S(1)} %get-tuple-element.290, f32[4,512,256]{2,1,0:T(8,128)S(1)} %fusion.17), kind=kCustom, calls=%fused_computation.4.clone.1 | custom fusion | flops 524288 | bytes 6291472 | tf_op jit(solution)/shard_map/while/body/eval_jaxpr/scatter-add | solution.py:49
  238.2 51.0 %reduce-scatter.5.cloned.1.call-done = f32[1024,256]{1,0:T(8,128)} async-done(((f32[8192,256]{1,0:T(8,128)}), f32[1024,256]{1,0:T(8,128)}) %reduce-scatter.5.cloned.1.call-update) | async-done | bytes 1048592 | tf_op jit(solution)/shard_map/reduce_scatter | solution.py:108
  291.6 111.7 %reduce-scatter.3.cloned.1.call-done = f32[1024,256]{1,0:T(8,128)} async-done(((f32[16384,256]{1,0:T(8,128)}), f32[1024,256]{1,0:T(8,128)}) %reduce-scatter.3.cloned.1.call-update) | async-done | bytes 1048592 | tf_op jit(solution)/shard_map/reduce_scatter | solution.py:105
  (128 shorter events, 47.6 us)
Async XLA Ops:
  7.2 4.4 %copy-start.3 = (bf16[1024]{0:T(1024)(128)(2,1)S(1)}, bf16[1024]{0:T(1024)(128)(2,1)}, u32[]{:S(2)}) copy-start(bf16[1024]{0:T(1024)(128)(2,1)} %param.18) | copy-start | bytes 6148
  7.2 41.0 %copy-start.6 = (s32[16]{0:T(128)S(1)}, s32[16]{0:T(128)}, u32[]{:S(2)}) copy-start(s32[16]{0:T(128)} %param.14) | copy-start | bytes 196
  7.2 41.0 %copy-start.5 = (s32[16]{0:T(128)S(1)}, s32[16]{0:T(128)}, u32[]{:S(2)}) copy-start(s32[16]{0:T(128)} %param.13) | copy-start | bytes 196
  7.2 46.7 %copy-start.4 = (bf16[1024]{0:T(1024)(128)(2,1)S(1)}, bf16[1024]{0:T(1024)(128)(2,1)}, u32[]{:S(2)}) copy-start(bf16[1024]{0:T(1024)(128)(2,1)} %param.21) | copy-start | bytes 6148
  7.2 73.5 %all-gather.5.cloned.1.call-start = ((), (), s32[]{:S(2)}) async-start(), calls=%async_computation.3 | async-start | bytes 4718592 | tf_op jit(solution)/shard_map/all_gather | solution.py:77
  9.3 109.7 %all-gather.3.cloned.1.call-start = ((), (), s32[]{:S(2)}) async-start(), calls=%async_computation.2 | async-start | bytes 8912896 | tf_op jit(solution)/shard_map/all_gather | solution.py:79
  11.5 277.7 %reduce-scatter.5.cloned.1.call-start = ((), (), s32[]{:S(2)}) async-start(), calls=%async_computation.5 | async-start | bytes 9437184 | tf_op jit(solution)/shard_map/reduce_scatter | solution.py:108
  11.6 7.8 %collective-permute-start = (bf16[1024]{0:T(1024)(128)(2,1)S(1)}, bf16[1024]{0:T(1024)(128)(2,1)S(1)}, u32[]{:S(2)}, u32[]{:S(2)}) collective-permute-start(bf16[1024]{0:T(1024)(128)(2,1)S(1)} %copy-done.3), channel_id=1, source_target_pairs={{0,8},{8,16},{16,24},{24,32},{32,40},{40,48},{48,56},{56,64},{64,7... | collective-permute-start | bytes 6152 | tf_op jit(solution)/shard_map/ppermute | solution.py:85
  19.4 5.8 %collective-permute-start.1 = (bf16[1024]{0:T(1024)(128)(2,1)S(1)}, bf16[1024]{0:T(1024)(128)(2,1)S(1)}, u32[]{:S(2)}, u32[]{:S(2)}) collective-permute-start(bf16[1024]{0:T(1024)(128)(2,1)S(1)} %collective-permute-done), channel_id=1, source_target_pairs={{0,8},{8,16},{16,24},{24,32},{32,40},{40,48},{48,56},{56,64},{64,7... | collective-permute-start | bytes 6152 | tf_op jit(solution)/shard_map/ppermute | solution.py:85
  19.4 5.8 %collective-permute-start.8 = (bf16[1024]{0:T(1024)(128)(2,1)S(1)}, bf16[1024]{0:T(1024)(128)(2,1)S(1)}, u32[]{:S(2)}, u32[]{:S(2)}) collective-permute-start(bf16[1024]{0:T(1024)(128)(2,1)S(1)} %copy-done.3), channel_id=1, source_target_pairs={{0,120},{8,0},{16,8},{24,16},{32,24},{40,32},{48,40},{56,48},{64,5... | collective-permute-start | bytes 6152 | tf_op jit(solution)/shard_map/ppermute | solution.py:88
  25.1 5.8 %collective-permute-start.2 = (bf16[1024]{0:T(1024)(128)(2,1)S(1)}, bf16[1024]{0:T(1024)(128)(2,1)S(1)}, u32[]{:S(2)}, u32[]{:S(2)}) collective-permute-start(bf16[1024]{0:T(1024)(128)(2,1)S(1)} %collective-permute-done.1), channel_id=1, source_target_pairs={{0,8},{8,16},{16,24},{24,32},{32,40},{40,48},{48,56},{56,64},{64,7... | collective-permute-start | bytes 6152 | tf_op jit(solution)/shard_map/ppermute | solution.py:85
  25.1 5.8 %collective-permute-start.9 = (bf16[1024]{0:T(1024)(128)(2,1)S(1)}, bf16[1024]{0:T(1024)(128)(2,1)S(1)}, u32[]{:S(2)}, u32[]{:S(2)}) collective-permute-start(bf16[1024]{0:T(1024)(128)(2,1)S(1)} %collective-permute-done.8), channel_id=1, source_target_pairs={{0,120},{8,0},{16,8},{24,16},{32,24},{40,32},{48,40},{56,48},{64,5... | collective-permute-start | bytes 6152 | tf_op jit(solution)/shard_map/ppermute | solution.py:88
  30.9 5.8 %collective-permute-start.3 = (bf16[1024]{0:T(1024)(128)(2,1)S(1)}, bf16[1024]{0:T(1024)(128)(2,1)S(1)}, u32[]{:S(2)}, u32[]{:S(2)}) collective-permute-start(bf16[1024]{0:T(1024)(128)(2,1)S(1)} %collective-permute-done.2), channel_id=1, source_target_pairs={{0,8},{8,16},{16,24},{24,32},{32,40},{40,48},{48,56},{56,64},{64,7... | collective-permute-start | bytes 6152 | tf_op jit(solution)/shard_map/ppermute | solution.py:85
  30.9 5.8 %collective-permute-start.10 = (bf16[1024]{0:T(1024)(128)(2,1)S(1)}, bf16[1024]{0:T(1024)(128)(2,1)S(1)}, u32[]{:S(2)}, u32[]{:S(2)}) collective-permute-start(bf16[1024]{0:T(1024)(128)(2,1)S(1)} %collective-permute-done.9), channel_id=1, source_target_pairs={{0,120},{8,0},{16,8},{24,16},{32,24},{40,32},{48,40},{56,48},{64,5... | collective-permute-start | bytes 6152 | tf_op jit(solution)/shard_map/ppermute | solution.py:88
  36.6 5.8 %collective-permute-start.4 = (bf16[1024]{0:T(1024)(128)(2,1)S(1)}, bf16[1024]{0:T(1024)(128)(2,1)S(1)}, u32[]{:S(2)}, u32[]{:S(2)}) collective-permute-start(bf16[1024]{0:T(1024)(128)(2,1)S(1)} %collective-permute-done.3), channel_id=1, source_target_pairs={{0,8},{8,16},{16,24},{24,32},{32,40},{40,48},{48,56},{56,64},{64,7... | collective-permute-start | bytes 6152 | tf_op jit(solution)/shard_map/ppermute | solution.py:85
  36.6 5.8 %collective-permute-start.11 = (bf16[1024]{0:T(1024)(128)(2,1)S(1)}, bf16[1024]{0:T(1024)(128)(2,1)S(1)}, u32[]{:S(2)}, u32[]{:S(2)}) collective-permute-start(bf16[1024]{0:T(1024)(128)(2,1)S(1)} %collective-permute-done.10), channel_id=1, source_target_pairs={{0,120},{8,0},{16,8},{24,16},{32,24},{40,32},{48,40},{56,48},{64,5... | collective-permute-start | bytes 6152 | tf_op jit(solution)/shard_map/ppermute | solution.py:88
  42.4 5.8 %collective-permute-start.5 = (bf16[1024]{0:T(1024)(128)(2,1)S(1)}, bf16[1024]{0:T(1024)(128)(2,1)S(1)}, u32[]{:S(2)}, u32[]{:S(2)}) collective-permute-start(bf16[1024]{0:T(1024)(128)(2,1)S(1)} %collective-permute-done.4), channel_id=1, source_target_pairs={{0,8},{8,16},{16,24},{24,32},{32,40},{40,48},{48,56},{56,64},{64,7... | collective-permute-start | bytes 6152 | tf_op jit(solution)/shard_map/ppermute | solution.py:85
  42.4 5.8 %collective-permute-start.12 = (bf16[1024]{0:T(1024)(128)(2,1)S(1)}, bf16[1024]{0:T(1024)(128)(2,1)S(1)}, u32[]{:S(2)}, u32[]{:S(2)}) collective-permute-start(bf16[1024]{0:T(1024)(128)(2,1)S(1)} %collective-permute-done.11), channel_id=1, source_target_pairs={{0,120},{8,0},{16,8},{24,16},{32,24},{40,32},{48,40},{56,48},{64,5... | collective-permute-start | bytes 6152 | tf_op jit(solution)/shard_map/ppermute | solution.py:88
  48.1 5.8 %collective-permute-start.6 = (bf16[1024]{0:T(1024)(128)(2,1)S(1)}, bf16[1024]{0:T(1024)(128)(2,1)S(1)}, u32[]{:S(2)}, u32[]{:S(2)}) collective-permute-start(bf16[1024]{0:T(1024)(128)(2,1)S(1)} %collective-permute-done.5), channel_id=1, source_target_pairs={{0,8},{8,16},{16,24},{24,32},{32,40},{40,48},{48,56},{56,64},{64,7... | collective-permute-start | bytes 6152 | tf_op jit(solution)/shard_map/ppermute | solution.py:85
  48.2 26.2 %collective-permute-start.13 = (bf16[1024]{0:T(1024)(128)(2,1)S(1)}, bf16[1024]{0:T(1024)(128)(2,1)S(1)}, u32[]{:S(2)}, u32[]{:S(2)}) collective-permute-start(bf16[1024]{0:T(1024)(128)(2,1)S(1)} %collective-permute-done.12), channel_id=1, source_target_pairs={{0,120},{8,0},{16,8},{24,16},{32,24},{40,32},{48,40},{56,48},{64,5... | collective-permute-start | bytes 6152 | tf_op jit(solution)/shard_map/ppermute | solution.py:88
  53.9 25.8 %collective-permute-start.7 = (bf16[1024]{0:T(1024)(128)(2,1)S(1)}, bf16[1024]{0:T(1024)(128)(2,1)S(1)}, u32[]{:S(2)}, u32[]{:S(2)}) collective-permute-start(bf16[1024]{0:T(1024)(128)(2,1)S(1)} %collective-permute-done.6), channel_id=1, source_target_pairs={{0,8},{8,16},{16,24},{24,32},{32,40},{40,48},{48,56},{56,64},{64,7... | collective-permute-start | bytes 6152 | tf_op jit(solution)/shard_map/ppermute | solution.py:85
  74.4 6.0 %collective-permute-start.14 = (bf16[1024]{0:T(1024)(128)(2,1)S(1)}, bf16[1024]{0:T(1024)(128)(2,1)S(1)}, u32[]{:S(2)}, u32[]{:S(2)}) collective-permute-start(bf16[1024]{0:T(1024)(128)(2,1)S(1)} %collective-permute-done.13), channel_id=1, source_target_pairs={{0,120},{8,0},{16,8},{24,16},{32,24},{40,32},{48,40},{56,48},{64,5... | collective-permute-start | bytes 6152 | tf_op jit(solution)/shard_map/ppermute | solution.py:88
  237.6 165.6 %reduce-scatter.3.cloned.1.call-start = ((), (), s32[]{:S(2)}) async-start(), calls=%async_computation.4 | async-start | bytes 17825792 | tf_op jit(solution)/shard_map/reduce_scatter | solution.py:105
  237.7 51.5 %copy-start = (f32[1024,256]{1,0:T(8,128)S(1)}, f32[1024,256]{1,0:T(8,128)}, u32[]{:S(2)}) copy-start(f32[1024,256]{1,0:T(8,128)} %param.19) | copy-start | bytes 3145732
  237.7 51.5 %copy-start.2 = (f32[1024,256]{1,0:T(8,128)S(1)}, f32[1024,256]{1,0:T(8,128)}, u32[]{:S(2)}) copy-start(f32[1024,256]{1,0:T(8,128)} %param.20) | copy-start | bytes 3145732
  238.2 165.0 %copy-start.1 = (f32[1024,256]{1,0:T(8,128)S(1)}, f32[1024,256]{1,0:T(8,128)}, u32[]{:S(2)}) copy-start(f32[1024,256]{1,0:T(8,128)} %param.16) | copy-start | bytes 3145732
Sparse Core Ops, SparseCore 0:
  10.3 35.6 all-gather.4
  48.7 70.2 all-gather.2
  237.7 51.3 reduce-scatter.4
  292.4 110.7 reduce-scatter.2
